TPU v7x, 32 devices: a whole 2x2x4 slice. The times are simulated.
32 devices in a mesh: ctx: 16 (over z, x, core), tp: 2 (over y).
Axes of the slice: x: 2, y: 2, z: 4, core: 2. Of those that a mesh axis runs over, the one named last changes fastest.
Arguments:
- queries: bfloat16 [16384, 4096], P('ctx', 'tp'), may hold values from -96 to 96
- rotated_key_rows: bfloat16 [16384, 2048], P('ctx', 'tp'), may hold values from -5 to 5
- value_head_rows: bfloat16 [16384, 2048], P('ctx', 'tp'), may hold values from -5 to 5
- w_out: bfloat16 [16, 256, 3840], P('tp', 'ctx'), may hold values from -0.09375 to 0.09375
- post_gain: float32 [3840], replicated, may hold values from 0.25 to 1.75
- doc_lengths: int32 [16], replicated, may hold values from 1 to 4096, 16384 in all
Outputs:
- normed_out: bfloat16 [16384, 3840], P(('ctx', 'tp'))
All inputs are finite; a program needn't handle non-finite values.
Results may differ from a plain program's by a relative error of at most 0.0085.
Values may be sent and summed in bfloat16 or wider, within the bound.
No kernel may reach another device: no remote copies, remote signals or barrier semaphores. Data moves between devices by JAX's collectives and lax.ppermute only.
A program may use at most 192 MiB of HBM per device.

v0:
```python
import jax
import jax.numpy as jnp
from jax import lax
from jax.sharding import PartitionSpec as P

HEAD_SIZE = 256
ATTEND_WINDOW = 1024


def shifted(shard, axis, by):
    devices = lax.axis_size(axis)
    pairs = [(i, i + by) for i in range(devices) if 0 <= i + by < devices]
    return lax.ppermute(shard, axis, pairs)


def post_norm(summed, post_gain):
    mean_sq = jnp.mean(summed * summed, axis=-1, keepdims=True)
    return (summed * lax.rsqrt(mean_sq + 1e-06) * post_gain).astype(jnp.bfloat16)


def score_part(query_block, key_portion, kv_heads, scaling):
    key_block = key_portion.reshape(key_portion.shape[0], kv_heads, HEAD_SIZE)
    return (
        jnp.einsum("qhgd,khd->hgqk", query_block, key_block, preferred_element_type=jnp.float32)
        * scaling
    )


def on_device(queries, rotated_key_rows, value_head_rows, w_out, post_gain, doc_lengths):
    tok_local = queries.shape[0]
    kv_heads = rotated_key_rows.shape[1] // HEAD_SIZE
    heads_local = queries.shape[1] // HEAD_SIZE
    head_groups = heads_local // kv_heads
    scaling = HEAD_SIZE ** (-0.5)
    query_block_size = min(512, tok_local)
    key_block_size = ATTEND_WINDOW + query_block_size
    block_total = tok_local // query_block_size
    query_blocks = [
        queries[b * query_block_size : (b + 1) * query_block_size].reshape(
            query_block_size, kv_heads, head_groups, HEAD_SIZE
        )
        for b in range(block_total)
    ]
    key_parts = []
    val_parts = []
    arrived = shifted((rotated_key_rows, value_head_rows), "ctx", 1)
    key_parts.insert(0, arrived[0])
    val_parts.insert(0, arrived[1])
    halo_keys = key_parts[0]
    all_vals = jnp.concatenate(val_parts + [value_head_rows], axis=0)
    base = lax.axis_index("ctx") * tok_local
    qpos_all = base + jnp.arange(tok_local, dtype=jnp.int32)
    kpos_all = base - ATTEND_WINDOW + jnp.arange(ATTEND_WINDOW + tok_local, dtype=jnp.int32)
    doc_ends = jnp.cumsum(doc_lengths)
    qdoc_all = jnp.sum((doc_ends[None, :] <= qpos_all[:, None]).astype(jnp.int32), axis=1)
    kdoc_all = jnp.sum((doc_ends[None, :] <= kpos_all[:, None]).astype(jnp.int32), axis=1)
    outputs = []
    for block_id in range(block_total):
        lower = block_id * query_block_size
        local_lo = max(lower, ATTEND_WINDOW) - ATTEND_WINDOW
        local_hi = lower + key_block_size - ATTEND_WINDOW
        local_scores = score_part(
            query_blocks[block_id], rotated_key_rows[local_lo:local_hi], kv_heads, scaling
        )
        halo_scores = score_part(
            query_blocks[block_id], halo_keys[lower:ATTEND_WINDOW], kv_heads, scaling
        )
        scores = jnp.concatenate([halo_scores, local_scores], axis=-1)
        value_block = all_vals[lower : lower + key_block_size].reshape(
            key_block_size, kv_heads, HEAD_SIZE
        )
        qpos = qpos_all[lower : lower + query_block_size]
        kpos = kpos_all[lower : lower + key_block_size]
        qdoc = qdoc_all[lower : lower + query_block_size]
        kdoc = kdoc_all[lower : lower + key_block_size]
        allowed = (
            (kpos[None, :] >= 0)
            & (kpos[None, :] <= qpos[:, None])
            & (qpos[:, None] - kpos[None, :] < ATTEND_WINDOW)
            & (kdoc[None, :] == qdoc[:, None])
        )
        scores = jnp.where(allowed[None, None], scores, -jnp.inf)
        top = jnp.max(scores, axis=-1, keepdims=True)
        expo = jnp.exp(scores - top)
        weights = (expo / jnp.sum(expo, axis=-1, keepdims=True)).astype(jnp.bfloat16)
        result = jnp.einsum(
            "hgqk,khd->qhgd", weights, value_block, preferred_element_type=jnp.float32
        )
        outputs.append(
            result.reshape(query_block_size, heads_local * HEAD_SIZE).astype(jnp.bfloat16)
        )
    attn = jnp.concatenate(outputs, axis=0).reshape(tok_local, heads_local, HEAD_SIZE)
    partial_value = jnp.einsum(
        "thn,hnd->td",
        attn,
        lax.all_gather(w_out, "ctx", axis=1, tiled=True),
        preferred_element_type=jnp.float32,
    )
    mine = lax.psum_scatter(
        partial_value.astype(jnp.bfloat16), "tp", scatter_dimension=0, tiled=True
    ).astype(jnp.float32)
    return post_norm(mine, post_gain)


def solution(mesh):
    placed = (P("ctx", "tp"), P("ctx", "tp"), P("ctx", "tp"), P("tp", "ctx", None), P(), P())
    return jax.shard_map(
        on_device, mesh=mesh, in_specs=placed, out_specs=P(("ctx", "tp"), None), check_vma=False
    )
```

profile of v0, /device:TPU:0, one launch (start us, length us, event | category | flops | bytes accessed | tf_op | source)
XLA Modules:
  0.0 379.6 jit_solution(13983909736662050847)
XLA Ops:
  6.5 0.0 copy-start.2
  6.5 0.0 all-gather.2.cloned.1.call-start
  6.5 0.7 all-gather.2.cloned.1.call-update
  7.3 0.0 reduce-scatter.2.cloned.1.call-start
  7.3 4.0 %copy.36 = bf16[1024,1024]{0,1:T(8,128)(2,1)} copy(bf16[1024,1024]{1,0:T(8,128)(2,1)} %param.7) | data formatting | bytes 4194304 | tf_op args[1]
  11.3 0.0 copy-start.8
  11.3 3.8 %collective-permute-start.1 = (bf16[1024,1024]{0,1:T(8,128)(2,1)}, bf16[1024,1024]{0,1:T(8,128)(2,1)}, u32[]{:S(2)}, u32[]{:S(2)}) collective-permute-start(bf16[1024,1024]{0,1:T(8,128)(2,1)} %copy.36), channel_id=1, source_target_pairs={{0,2},{2,4},{4,6},{6,8},{8,10},{10,12},{12,14},{14,16},{16,18},{18... | collective-permute-start | bytes 6291464 | tf_op jit(solution)/shard_map/ppermute | solution.py:13
  15.1 4.5 %collective-permute-start = (bf16[1024,1024]{1,0:T(8,128)(2,1)}, bf16[1024,1024]{1,0:T(8,128)(2,1)}, u32[]{:S(2)}, u32[]{:S(2)}) collective-permute-start(bf16[1024,1024]{1,0:T(8,128)(2,1)} %param.8), channel_id=1, source_target_pairs={{0,2},{2,4},{4,6},{6,8},{8,10},{10,12},{12,14},{14,16},{16,18},{18... | collective-permute-start | bytes 6291464 | tf_op jit(solution)/shard_map/ppermute | solution.py:13
  19.6 1.4 slice.59
  21.0 0.0 copy-done.2
  21.0 2.8 reshape.281
  23.8 0.0 copy-done.8
  23.8 0.1 copy.35
  24.0 0.1 reduce
  24.1 4.0 %fusion.26 = (bf16[512,2048]{1,0:T(8,128)(2,1)S(1)}, bf16[512,2048]{1,0:T(8,128)(2,1)}) fusion(bf16[1024,2048]{1,0:T(8,128)(2,1)} %param.6), kind=kLoop, calls=%fused_computation.50 | loop fusion | bytes 8388608 | tf_op jit(solution)/shard_map/slice | solution.py:39
  28.1 2.5 copy.73
  30.6 2.9 copy.74
  33.5 0.1 convert_reduce_fusion.1
  33.6 0.1 convert_reduce_fusion
  33.8 2.6 fusion.17
  36.4 2.6 fusion.19
  38.9 0.0 copy-start.1
  38.9 6.4 %multiply_bitcast_fusion.3 = f32[4,2,512,512]{2,3,1,0:T(8,128)} fusion(bf16[512,4,256,1]{0,2,3,1:T(8,128)(2,1)S(1)} %bitcast.60, bf16[512,4,2,256]{0,3,2,1:T(8,128)(2,1)} %bitcast.57), kind=kOutput, calls=%fused_computation.22 | convolution fusion | flops 1075838976 | bytes 11534336 | tf_op jit(solution)/shard_map/qhgd,khd->hgqk/dot_general | solution.py:24
  45.3 0.0 copy-done.1
  45.3 8.0 %multiply_bitcast_fusion = f32[4,2,512,1024]{2,3,1,0:T(8,128)} fusion(bf16[512,4,2,256]{0,3,2,1:T(8,128)(2,1)S(1)} %bitcast.55, bf16[1024,4,256,1]{2,1,0,3:T(4,128)(2,1)S(1)} %bitcast.59), kind=kOutput, calls=%fused_computation.10 | convolution fusion | flops 2151677952 | bytes 20971520 | tf_op jit(solution)/shard_map/qhgd,khd->hgqk/dot_general | solution.py:24
  53.4 0.0 copy-start.4
  53.4 0.0 collective-permute-done
  53.4 1.9 constant_dynamic-update-slice_fusion.1
  55.3 0.3 copy-done.4
  55.6 0.2 constant_dynamic-update-slice_fusion
  55.8 3.5 fusion.27
  59.3 4.7 %copy.34 = bf16[1536,1024]{0,1:T(8,128)(2,1)} copy(bf16[1536,1024]{1,0:T(8,128)(2,1)} %get-tuple-element.7) | data formatting | bytes 6291456 | tf_op jit(solution)/shard_map/slice | solution.py:69
  63.9 0.0 collective-permute-done.1
  63.9 0.0 copy-start.6
  63.9 4.7 %multiply_bitcast_fusion.1 = f32[4,2,512,1024]{2,3,1,0:T(8,128)S(1)} fusion(bf16[1024,4,256,1]{0,2,3,1:T(8,128)(2,1)} %bitcast.28, bf16[512,4,2,256]{0,3,2,1:T(8,128)(2,1)} %bitcast.58), kind=kOutput, calls=%fused_computation.11 | convolution fusion | flops 2151677952 | bytes 20971520 | tf_op jit(solution)/shard_map/qhgd,khd->hgqk/dot_general | solution.py:24
  68.6 0.0 copy-done.6
  68.6 14.9 %fusion.33 = (f32[4,2,512]{2,1,0:T(2,128)S(1)}, f32[4,2,512,1536]{2,3,1,0:T(8,128)}) fusion(f32[4,2,512,512]{2,3,1,0:T(8,128)} %multiply_bitcast_fusion.3, f32[4,2,512,1024]{2,3,1,0:T(8,128)S(1)} %multiply_bitcast_fusion.1, pred[512,1536]{0,1:T(8,128)(4,1)S(1)} %copy-done.6), kind=kOutput, calls=%fused_computation.57 | output fusion | flops 25167360 | bytes 51134464 | tf_op jit(solution)/shard_map/sub | solution.py:84
  83.5 14.1 %fusion.22 = bf16[4,256,2,512]{3,1,2,0:T(8,128)(2,1)} fusion(bf16[1536,4,256,1]{0,2,3,1:T(8,128)(2,1)} %bitcast.62, f32[4,2,512,1536]{2,3,1,0:T(8,128)} %get-tuple-element.22, f32[4,2,512]{2,1,0:T(2,128)S(1)} %get-tuple-element.21), kind=kOutput, calls=%fused_computation.37 | convolution fusion | flops 3234856960 | bytes 30425088 | tf_op jit(solution)/shard_map/hgqk,khd->qhgd/dot_general | solution.py:86
  97.6 3.9 %copy.51 = bf16[512,8,256]{2,0,1:T(8,128)(2,1)} copy(bf16[512,8,256]{0,2,1:T(8,128)(2,1)} %bitcast.64) | data formatting | bytes 4194304 | tf_op jit(solution)/shard_map/convert_element_type | solution.py:90
  101.6 4.6 %copy.44 = bf16[1536,1024]{0,1:T(8,128)(2,1)} copy(bf16[1536,1024]{1,0:T(8,128)(2,1)} %get-tuple-element.8) | data formatting | bytes 6291456 | tf_op jit(solution)/shard_map/slice | solution.py:69
  106.2 1.3 slice.63
  107.5 4.6 %multiply_bitcast_fusion.2 = f32[4,2,512,512]{2,3,1,0:T(8,128)} fusion(bf16[512,4,256,1]{0,2,3,1:T(8,128)(2,1)S(1)} %bitcast.61, bf16[512,4,2,256]{0,3,2,1:T(8,128)(2,1)S(1)} %bitcast.56), kind=kOutput, calls=%fused_computation.21 | convolution fusion | flops 1075838976 | bytes 11534336 | tf_op jit(solution)/shard_map/qhgd,khd->hgqk/dot_general | solution.py:24
  112.1 0.0 copy-start.3
  112.1 16.7 %fusion.32 = (f32[4,2,512]{2,1,0:T(2,128)S(1)}, f32[4,2,512,1536]{2,3,1,0:T(8,128)}) fusion(f32[4,2,512,1024]{2,3,1,0:T(8,128)} %multiply_bitcast_fusion, f32[4,2,512,512]{2,3,1,0:T(8,128)} %multiply_bitcast_fusion.2, pred[512,1536]{0,1:T(8,128)(4,1)} %fusion.19), kind=kOutput, calls=%fused_computation.56 | output fusion | flops 25167360 | bytes 51134464 | tf_op jit(solution)/shard_map/sub | solution.py:84
  128.8 0.0 copy-done.3
  128.8 13.1 %fusion.21 = bf16[4,256,2,512]{3,1,2,0:T(8,128)(2,1)} fusion(bf16[1536,4,256,1]{0,2,3,1:T(8,128)(2,1)S(1)} %bitcast.63, f32[4,2,512,1536]{2,3,1,0:T(8,128)} %get-tuple-element.20, f32[4,2,512]{2,1,0:T(2,128)S(1)} %get-tuple-element.19), kind=kOutput, calls=%fused_computation.36 | convolution fusion | flops 3234856960 | bytes 30425088 | tf_op jit(solution)/shard_map/hgqk,khd->qhgd/dot_general | solution.py:86
  141.9 0.0 copy-start.5
  141.9 4.1 %copy.52 = bf16[512,8,256]{2,0,1:T(8,128)(2,1)} copy(bf16[512,8,256]{0,2,1:T(8,128)(2,1)} %bitcast.65) | data formatting | bytes 4194304 | tf_op jit(solution)/shard_map/convert_element_type | solution.py:90
  145.9 15.4 %all-gather.2.cloned.1.call-done = bf16[8,256,3840]{2,1,0:T(8,128)(2,1)} async-done(((bf16[8,16,3840]{2,1,0:T(8,128)(2,1)}), bf16[8,256,3840]{2,1,0:T(8,128)(2,1)}) %all-gather.2.cloned.1.call-update) | async-done | bytes 15728656 | tf_op jit(solution)/shard_map/all_gather | solution.py:96
  161.3 0.0 copy-done.5
  161.3 21.5 %bitcast_convert_fusion = bf16[1024,3840]{1,0:T(8,128)(2,1)} fusion(bf16[8,256,3840]{2,1,0:T(8,128)(2,1)} %all-gather.2.cloned.1.call-done, bf16[512,8,256]{2,0,1:T(8,128)(2,1)} %copy.52, bf16[512,8,256]{2,0,1:T(8,128)(2,1)S(1)} %copy-done.5), kind=kOutput, calls=%fused_computation.12 | convolution fusion | flops 16118448128 | bytes 27787264 | tf_op jit(solution)/shard_map/thn,hnd->td/dot_general | solution.py:93
  182.8 0.0 copy-start.7
  182.8 0.0 reduce-scatter.2.cloned.1.call-update
  182.8 183.3 %reduce-scatter.2.cloned.1.call-done = bf16[512,3840]{1,0:T(8,128)(2,1)} async-done(((bf16[1024,3840]{1,0:T(8,128)(2,1)}), bf16[512,3840]{1,0:T(8,128)(2,1)}) %reduce-scatter.2.cloned.1.call-update) | async-done | bytes 3932176 | tf_op jit(solution)/shard_map/reduce_scatter | solution.py:99
  366.1 0.0 copy-start
  366.1 3.1 fusion.10
  369.3 0.0 copy-done.7
  369.3 0.2 copy-done
  369.4 3.3 fusion.12
  (7 shorter events, 0.1 us)
Async XLA Ops:
  6.5 14.5 %copy-start.2 = (bf16[1024,1024]{1,0:T(8,128)(2,1)S(1)}, bf16[1024,1024]{1,0:T(8,128)(2,1)}, u32[]{:S(2)}) copy-start(bf16[1024,1024]{1,0:T(8,128)(2,1)} %param.7) | copy-start | bytes 6291460
  6.5 154.8 %all-gather.2.cloned.1.call-start = ((), (), s32[]{:S(2)}) async-start(), calls=%async_computation.1 | async-start | bytes 16711680 | tf_op jit(solution)/shard_map/all_gather | solution.py:96
  7.3 358.9 %reduce-scatter.2.cloned.1.call-start = ((), (), s32[]{:S(2)}) async-start(), calls=%async_computation.2 | async-start | bytes 11796480 | tf_op jit(solution)/shard_map/reduce_scatter | solution.py:99
  11.3 12.6 %copy-start.8 = (s32[16]{0:T(128)S(1)}, s32[16]{0:T(128)}, u32[]{:S(2)}) copy-start(s32[16]{0:T(128)} %param.11) | copy-start | bytes 196
  11.3 52.7 %collective-permute-start.1 = (bf16[1024,1024]{0,1:T(8,128)(2,1)}, bf16[1024,1024]{0,1:T(8,128)(2,1)}, u32[]{:S(2)}, u32[]{:S(2)}) collective-permute-start(bf16[1024,1024]{0,1:T(8,128)(2,1)} %copy.36), channel_id=1, source_target_pairs={{0,2},{2,4},{4,6},{6,8},{8,10},{10,12},{12,14},{14,16},{16,18},{18... | collective-permute-start | bytes 6291464 | tf_op jit(solution)/shard_map/ppermute | solution.py:13
  15.1 38.3 %collective-permute-start = (bf16[1024,1024]{1,0:T(8,128)(2,1)}, bf16[1024,1024]{1,0:T(8,128)(2,1)}, u32[]{:S(2)}, u32[]{:S(2)}) collective-permute-start(bf16[1024,1024]{1,0:T(8,128)(2,1)} %param.8), channel_id=1, source_target_pairs={{0,2},{2,4},{4,6},{6,8},{8,10},{10,12},{12,14},{14,16},{16,18},{18... | collective-permute-start | bytes 6291464 | tf_op jit(solution)/shard_map/ppermute | solution.py:13
  38.9 6.4 %copy-start.1 = (bf16[1024,4,256]{2,1,0:T(4,128)(2,1)S(1)}, bf16[1024,4,256]{2,1,0:T(4,128)(2,1)}, u32[]{:S(2)}) copy-start(bf16[1024,4,256]{2,1,0:T(4,128)(2,1)} %reshape.281) | copy-start | bytes 6291460
  53.4 2.2 copy-start.4
  63.9 4.7 %copy-start.6 = (pred[512,1536]{0,1:T(8,128)(4,1)S(1)}, pred[512,1536]{0,1:T(8,128)(4,1)}, u32[]{:S(2)}) copy-start(pred[512,1536]{0,1:T(8,128)(4,1)} %fusion.17) | copy-start | bytes 2359300
  112.1 16.7 %copy-start.3 = (bf16[1536,1024]{0,1:T(8,128)(2,1)S(1)}, bf16[1536,1024]{0,1:T(8,128)(2,1)}, u32[]{:S(2)}) copy-start(bf16[1536,1024]{0,1:T(8,128)(2,1)} %copy.44) | copy-start | bytes 9437188
  141.9 19.4 %copy-start.5 = (bf16[512,8,256]{2,0,1:T(8,128)(2,1)S(1)}, bf16[512,8,256]{2,0,1:T(8,128)(2,1)}, u32[]{:S(2)}) copy-start(bf16[512,8,256]{2,0,1:T(8,128)(2,1)} %copy.51) | copy-start | bytes 6291460
  182.8 186.4 %copy-start.7 = (f32[3840]{0:T(1024)S(1)}, f32[3840]{0:T(1024)}, u32[]{:S(2)}) copy-start(f32[3840]{0:T(1024)} %param.10) | copy-start | bytes 46084
  366.1 3.3 copy-start
Sparse Core Ops, SparseCore 0:
  9.6 151.6 all-gather.1
  183.0 183.1 reduce-scatter.1
where the time goes:
time: 380 us
  waiting for transfers between devices  199 us (52%)
  matrix products  72.4 us (19%)
  other arithmetic  43.5 us (11%)
  local copies, waits for them, and re-layouts  42.4 us (11%)
  between operations  13.5 us (4%)
  starting transfers between devices  8.37 us (2%)
    reduce_scatter x1, waiting for transfers between devices, on_device(): lax.psum_scatter(partial_value.astype(jnp.bfloat16), 'tp', scatter_dimens...  183 us
    sub x2, other arithmetic, on_device(): expo = jnp.exp(scores - top)  31.5 us
    dot_general x2, matrix products, on_device(): jnp.einsum('hgqk,khd->qhgd', weights, value_block, preferred_element_type...  27.2 us
    dot_general x4, matrix products, score_part(): jnp.einsum('qhgd,khd->hgqk', query_block, key_block, preferred_element_ty...  23.7 us
    dot_general x1, matrix products, on_device(): jnp.einsum('thn,hnd->td', attn, lax.all_gather(w_out, 'ctx', axis=1, tile...  21.5 us
    all_gather x1, waiting for transfers between devices, on_device(): lax.all_gather(w_out, 'ctx', axis=1, tiled=True)  15.4 us
    slice x3, local copies, waits for them, and re-layouts, on_device(): all_vals[lower:lower + key_block_size]  12.8 us
    unnamed x22, local copies, waits for them, and re-layouts  11.8 us
  transfers between devices with their start and end apart: 4, of which 2 were waited for; matrix products, arithmetic and copies ran while one was open for 34% of the time, Pallas kernels for 0%

commit v1 on v0

--- a/solution.py
+++ b/solution.py
@@ -2,6 +2,7 @@
 import jax.numpy as jnp
 from jax import lax
 from jax.sharding import PartitionSpec as P
+from jax.lax import axis_index, ppermute, psum
 
 HEAD_SIZE = 256
 ATTEND_WINDOW = 1024
@@ -90,10 +91,24 @@
             result.reshape(query_block_size, heads_local * HEAD_SIZE).astype(jnp.bfloat16)
         )
     attn = jnp.concatenate(outputs, axis=0).reshape(tok_local, heads_local, HEAD_SIZE)
+
+    def measure_tracks(peer_axis, array_in):
+        x_next = psum(1, peer_axis)
+        carry_in = axis_index(peer_axis)
+        base_arr, s_next = (x_next, carry_in)
+        piece_next, latest = (array_in, 1)
+        while latest < base_arr:
+            r2 = ppermute(piece_next, peer_axis, [(nth, nth ^ latest) for nth in range(base_arr)])
+            moved = jnp.concatenate([piece_next, r2], axis=1)
+            h_now = jnp.concatenate([r2, piece_next], axis=1)
+            piece_next = jnp.where(s_next & latest == 0, moved, h_now)
+            latest = 2 * latest
+        return piece_next
+
     partial_value = jnp.einsum(
         "thn,hnd->td",
         attn,
-        lax.all_gather(w_out, "ctx", axis=1, tiled=True),
+        measure_tracks("ctx", array_in=w_out),
         preferred_element_type=jnp.float32,
     )
     mine = lax.psum_scatter(

time: 380 us -> 678 us (1.78)
  waiting for transfers between devices: 199 us -> 453 us
  starting transfers between devices: 8.37 us -> 37.4 us
  other arithmetic: 43.5 us -> 57.4 us
    ppermute x0 -> x4, waiting for transfers between devices: none -> 358 us  [measure_tracks(): ppermute(piece_next, peer_axis, [(nth, nth ^ latest) for nth in range(bas...]
    reduce_scatter x1, waiting for transfers between devices: 183 us -> 94.9 us  [on_device(): lax.psum_scatter(partial_value.astype(jnp.bfloat16), 'tp', scatter_dimens...]
    ppermute x0 -> x4, starting transfers between devices: none -> 29 us  [measure_tracks(): ppermute(piece_next, peer_axis, [(nth, nth ^ latest) for nth in range(bas...]
    all_gather x1 -> x0, waiting for transfers between devices: 15.4 us -> none  [on_device(): lax.all_gather(w_out, 'ctx', axis=1, tiled=True)]
    select_n x0 -> x3, other arithmetic: none -> 15.3 us  [measure_tracks(): piece_next = jnp.where(s_next & latest == 0, moved, h_now)]
    unnamed x22 -> x26, local copies, waits for them, and re-layouts: 11.8 us -> 13.9 us
  transfers between devices with their start and end apart: 4 -> 7, of which waited for: 2 -> 4; matrix products, arithmetic and copies ran while one was open for 34% -> 19% of each run, Pallas kernels for 0% -> 0%
where the time goes in v1:
time: 678 us; the launch traced here: 677 us
  waiting for transfers between devices  453 us (67%)
  matrix products  71.4 us (11%)
  other arithmetic  57.4 us (8%)
  local copies, waits for them, and re-layouts  44.4 us (7%)
  starting transfers between devices  37.4 us (6%)
  between operations  13.6 us (2%)
    ppermute x4, waiting for transfers between devices, measure_tracks(): ppermute(piece_next, peer_axis, [(nth, nth ^ latest) for nth in range(bas...  358 us
    reduce_scatter x1, waiting for transfers between devices, on_device(): lax.psum_scatter(partial_value.astype(jnp.bfloat16), 'tp', scatter_dimens...  94.9 us
    sub x2, other arithmetic, on_device(): expo = jnp.exp(scores - top)  31 us
    ppermute x4, starting transfers between devices, measure_tracks(): ppermute(piece_next, peer_axis, [(nth, nth ^ latest) for nth in range(bas...  29 us
    dot_general x2, matrix products, on_device(): jnp.einsum('hgqk,khd->qhgd', weights, value_block, preferred_element_type...  26.8 us
    dot_general x1, matrix products, on_device(): jnp.einsum('thn,hnd->td', attn, measure_tracks('ctx', array_in=w_out), pr...  23.3 us
    dot_general x4, matrix products, score_part(): jnp.einsum('qhgd,khd->hgqk', query_block, key_block, preferred_element_ty...  21.4 us
    select_n x3, other arithmetic, measure_tracks(): piece_next = jnp.where(s_next & latest == 0, moved, h_now)  15.3 us
  transfers between devices with their start and end apart: 7, of which 4 were waited for; matrix products, arithmetic and copies ran while one was open for 19% of the time, Pallas kernels for 0%

profile of v1, /device:TPU:0, one launch (start us, length us, event | category | flops | bytes accessed | tf_op | source)
XLA Modules:
  0.0 677.1 jit_solution(4178885970770630075)
XLA Ops:
  6.5 0.0 copy-start.5
  6.5 0.0 reduce-scatter.2.cloned.1.call-start
  6.5 4.1 copy.36
  10.6 0.0 copy-start.10
  10.6 3.8 collective-permute-start.1
  14.5 4.5 collective-permute-start
  19.0 0.0 collective-permute-start.2
  19.0 1.3 slice.59
  20.3 0.0 copy-done.5
  20.3 2.8 reshape.281
  23.1 0.0 copy-done.10
  23.1 0.1 copy.35
  23.2 0.1 reduce
  23.3 4.0 fusion.33
  27.3 2.5 copy.73
  29.8 2.9 copy.74
  32.7 0.0 copy-start
  32.7 0.1 convert_reduce_fusion.1
  32.8 0.1 convert_reduce_fusion
  32.9 0.0 collective-permute-done.2
  32.9 2.7 maximum_select_fusion.10
  35.6 0.3 collective-permute-start.3
  36.0 1.7 fusion.24
  37.7 0.0 copy-done
  37.7 4.6 multiply_bitcast_fusion.3
  42.3 2.6 fusion.26
  44.9 36.0 %collective-permute-done.3 = bf16[8,32,3840]{2,1,0:T(8,128)(2,1)S(1)} collective-permute-done((bf16[8,32,3840]{2,1,0:T(8,128)(2,1)S(1)}, bf16[8,32,3840]{2,1,0:T(8,128)(2,1)S(1)}, u32[]{:S(2)}, u32[]{:S(2)}) %collective-permute-start.3) | collective-permute-done | bytes 1966112 | tf_op jit(solution)/shard_map/ppermute | solution.py:101
  80.9 2.4 maximum_select_fusion.9
  83.3 25.9 %collective-permute-start.4 = (bf16[8,64,3840]{2,1,0:T(8,128)(2,1)}, bf16[8,64,3840]{2,1,0:T(8,128)(2,1)}, u32[]{:S(2)}, u32[]{:S(2)}) collective-permute-start(bf16[8,64,3840]{2,1,0:T(8,128)(2,1)} %maximum_select_fusion.9), channel_id=1, source_target_pairs={{0,8},{2,10},{4,12},{6,14},{8,0},{10,2},{12,4},{14,6},{16,24},{18,... | collective-permute-start | bytes 11796488 | tf_op jit(solution)/shard_map/ppermute | solution.py:101
  109.2 0.0 copy-done.4
  109.2 8.2 %multiply_bitcast_fusion = f32[4,2,512,1024]{2,3,1,0:T(8,128)} fusion(bf16[512,4,2,256]{0,3,2,1:T(8,128)(2,1)S(1)} %bitcast.54, bf16[1024,4,256,1]{2,1,0,3:T(4,128)(2,1)S(1)} %bitcast.58), kind=kOutput, calls=%fused_computation.10 | convolution fusion | flops 2151677952 | bytes 20971520 | tf_op jit(solution)/shard_map/qhgd,khd->hgqk/dot_general | solution.py:25
  117.4 0.0 collective-permute-done
  117.4 1.9 constant_dynamic-update-slice_fusion.1
  119.3 0.3 copy-done.7
  119.6 0.2 constant_dynamic-update-slice_fusion
  119.8 0.0 copy-start.1
  119.8 0.0 collective-permute-done.1
  119.8 2.0 copy-done.1
  121.9 4.0 multiply_bitcast_fusion.1
  125.9 14.3 %fusion.40 = (f32[4,2,512]{2,1,0:T(2,128)S(1)}, f32[4,2,512,1536]{2,3,1,0:T(8,128)}) fusion(f32[4,2,512,512]{2,3,1,0:T(8,128)} %multiply_bitcast_fusion.3, f32[4,2,512,1024]{2,3,1,0:T(8,128)S(1)} %multiply_bitcast_fusion.1, pred[512,1536]{0,1:T(8,128)(4,1)S(1)} %fusion.24), kind=kOutput, calls=%fused_computation.68 | output fusion | flops 25167360 | bytes 51134464 | tf_op jit(solution)/shard_map/sub | solution.py:85
  140.2 54.5 %collective-permute-done.4 = bf16[8,64,3840]{2,1,0:T(8,128)(2,1)} collective-permute-done((bf16[8,64,3840]{2,1,0:T(8,128)(2,1)}, bf16[8,64,3840]{2,1,0:T(8,128)(2,1)}, u32[]{:S(2)}, u32[]{:S(2)}) %collective-permute-start.4) | collective-permute-done | bytes 3932192 | tf_op jit(solution)/shard_map/ppermute | solution.py:101
  194.7 10.3 %maximum_select_fusion.6 = bf16[8,128,3840]{2,1,0:T(8,128)(2,1)} fusion(bf16[8,64,3840]{2,1,0:T(8,128)(2,1)} %collective-permute-done.4, bf16[8,64,3840]{2,1,0:T(8,128)(2,1)} %maximum_select_fusion.9, pred[]{:T(512)S(6)} %eq.53), kind=kLoop, calls=%fused_computation.34 | loop fusion | flops 35389440 | bytes 15728641 | tf_op jit(solution)/shard_map/jit(_where)/select_n | solution.py:104
  205.0 2.8 collective-permute-start.5
  207.7 0.0 copy-done.2
  207.7 3.6 fusion.34
  211.3 4.7 copy.34
  216.0 13.9 %fusion.29 = bf16[4,256,2,512]{3,1,2,0:T(8,128)(2,1)} fusion(bf16[1536,4,256,1]{0,2,3,1:T(8,128)(2,1)} %bitcast.62, f32[4,2,512,1536]{2,3,1,0:T(8,128)} %get-tuple-element.22, f32[4,2,512]{2,1,0:T(2,128)S(1)} %get-tuple-element.21), kind=kOutput, calls=%fused_computation.48 | convolution fusion | flops 3234856960 | bytes 30425088 | tf_op jit(solution)/shard_map/hgqk,khd->qhgd/dot_general | solution.py:87
  229.9 3.9 copy.51
  233.8 4.6 copy.44
  238.4 1.3 slice.63
  239.7 4.5 multiply_bitcast_fusion.2
  244.3 16.7 %fusion.39 = (f32[4,2,512]{2,1,0:T(2,128)S(1)}, f32[4,2,512,1536]{2,3,1,0:T(8,128)}) fusion(f32[4,2,512,1024]{2,3,1,0:T(8,128)} %multiply_bitcast_fusion, f32[4,2,512,512]{2,3,1,0:T(8,128)} %multiply_bitcast_fusion.2, pred[512,1536]{0,1:T(8,128)(4,1)} %fusion.26), kind=kOutput, calls=%fused_computation.67 | output fusion | flops 25167360 | bytes 51134464 | tf_op jit(solution)/shard_map/sub | solution.py:85
  261.0 0.0 copy-done.6
  261.0 12.9 %fusion.28 = bf16[4,256,2,512]{3,1,2,0:T(8,128)(2,1)} fusion(bf16[1536,4,256,1]{0,2,3,1:T(8,128)(2,1)S(1)} %bitcast.61, f32[4,2,512,1536]{2,3,1,0:T(8,128)} %get-tuple-element.20, f32[4,2,512]{2,1,0:T(2,128)S(1)} %get-tuple-element.19), kind=kOutput, calls=%fused_computation.47 | convolution fusion | flops 3234856960 | bytes 30425088 | tf_op jit(solution)/shard_map/hgqk,khd->qhgd/dot_general | solution.py:87
  273.9 4.1 copy.52
  278.0 267.4 %collective-permute-done.5 = bf16[8,128,3840]{2,1,0:T(8,128)(2,1)} collective-permute-done((bf16[8,128,3840]{2,1,0:T(8,128)(2,1)}, bf16[8,128,3840]{2,1,0:T(8,128)(2,1)}, u32[]{:S(2)}, u32[]{:S(2)}) %collective-permute-start.5) | collective-permute-done | bytes 7864352 | tf_op jit(solution)/shard_map/ppermute | solution.py:101
  545.4 0.0 copy-done.8
  545.4 23.3 %bitcast_convert_fusion = bf16[1024,3840]{1,0:T(8,128)(2,1)} fusion(bf16[8,128,3840]{2,1,0:T(8,128)(2,1)} %collective-permute-done.5, bf16[8,128,3840]{2,1,0:T(8,128)(2,1)} %maximum_select_fusion.6, pred[]{:T(512)S(6)} %eq.52, bf16[512,8,256]{2,0,1:T(8,128)(2,1)} %copy.52, bf16[512,8,256]{2,0,1:T(8,128)(2,1)S(1)} %copy-done.8), kind=kOutput, calls=%fused_computation.19 | convolution fusion | flops 16189227008 | bytes 27787264 | tf_op jit(solution)/shard_map/thn,hnd->td/dot_general | solution.py:108
  568.7 0.0 reduce-scatter.2.cloned.1.call-update
  568.7 94.9 %reduce-scatter.2.cloned.1.call-done = bf16[512,3840]{1,0:T(8,128)(2,1)} async-done(((bf16[1024,3840]{1,0:T(8,128)(2,1)}), bf16[512,3840]{1,0:T(8,128)(2,1)}) %reduce-scatter.2.cloned.1.call-update) | async-done | bytes 3932176 | tf_op jit(solution)/shard_map/reduce_scatter | solution.py:114
  663.6 3.1 fusion.17
  666.7 0.0 copy-done.9
  666.7 0.2 copy-done.3
  666.9 3.3 fusion.19
  (14 shorter events, 0.1 us)
Async XLA Ops:
  6.5 13.8 %copy-start.5 = (bf16[1024,1024]{1,0:T(8,128)(2,1)S(1)}, bf16[1024,1024]{1,0:T(8,128)(2,1)}, u32[]{:S(2)}) copy-start(bf16[1024,1024]{1,0:T(8,128)(2,1)} %param.7) | copy-start | bytes 6291460
  6.5 657.1 %reduce-scatter.2.cloned.1.call-start = ((), (), s32[]{:S(2)}) async-start(), calls=%async_computation.1 | async-start | bytes 11796480 | tf_op jit(solution)/shard_map/reduce_scatter | solution.py:114
  10.6 12.5 %copy-start.10 = (s32[16]{0:T(128)S(1)}, s32[16]{0:T(128)}, u32[]{:S(2)}) copy-start(s32[16]{0:T(128)} %param.11) | copy-start | bytes 196
  10.6 109.2 %collective-permute-start.1 = (bf16[1024,1024]{0,1:T(8,128)(2,1)}, bf16[1024,1024]{0,1:T(8,128)(2,1)}, u32[]{:S(2)}, u32[]{:S(2)}) collective-permute-start(bf16[1024,1024]{0,1:T(8,128)(2,1)} %copy.36), channel_id=1, source_target_pairs={{0,2},{2,4},{4,6},{6,8},{8,10},{10,12},{12,14},{14,16},{16,18},{18... | collective-permute-start | bytes 6291464 | tf_op jit(solution)/shard_map/ppermute | solution.py:14
  14.5 103.0 %collective-permute-start = (bf16[1024,1024]{1,0:T(8,128)(2,1)}, bf16[1024,1024]{1,0:T(8,128)(2,1)}, u32[]{:S(2)}, u32[]{:S(2)}) collective-permute-start(bf16[1024,1024]{1,0:T(8,128)(2,1)} %param.8), channel_id=1, source_target_pairs={{0,2},{2,4},{4,6},{6,8},{8,10},{10,12},{12,14},{14,16},{16,18},{18... | collective-permute-start | bytes 6291464 | tf_op jit(solution)/shard_map/ppermute | solution.py:14
  19.0 13.9 %collective-permute-start.2 = (bf16[8,16,3840]{2,1,0:T(8,128)(2,1)}, bf16[8,16,3840]{2,1,0:T(8,128)(2,1)}, u32[]{:S(2)}, u32[]{:S(2)}) collective-permute-start(bf16[8,16,3840]{2,1,0:T(8,128)(2,1)} %param.9), channel_id=1, source_target_pairs={{0,2},{2,0},{4,6},{6,4},{8,10},{10,8},{12,14},{14,12},{16,18},{18,... | collective-permute-start | bytes 2949128 | tf_op jit(solution)/shard_map/ppermute | solution.py:101
  32.7 5.0 copy-start
  35.6 45.3 %collective-permute-start.3 = (bf16[8,32,3840]{2,1,0:T(8,128)(2,1)S(1)}, bf16[8,32,3840]{2,1,0:T(8,128)(2,1)S(1)}, u32[]{:S(2)}, u32[]{:S(2)}) collective-permute-start(bf16[8,32,3840]{2,1,0:T(8,128)(2,1)S(1)} %maximum_select_fusion.10), channel_id=1, source_target_pairs={{0,4},{2,6},{4,0},{6,2},{8,12},{10,14},{12,8},{14,10},{16,20},{18,... | collective-permute-start | bytes 5898248 | tf_op jit(solution)/shard_map/ppermute | solution.py:101
  42.3 66.9 %copy-start.4 = (bf16[1024,4,256]{2,1,0:T(4,128)(2,1)S(1)}, bf16[1024,4,256]{2,1,0:T(4,128)(2,1)}, u32[]{:S(2)}) copy-start(bf16[1024,4,256]{2,1,0:T(4,128)(2,1)} %reshape.281) | copy-start | bytes 6291460
  83.3 111.4 %collective-permute-start.4 = (bf16[8,64,3840]{2,1,0:T(8,128)(2,1)}, bf16[8,64,3840]{2,1,0:T(8,128)(2,1)}, u32[]{:S(2)}, u32[]{:S(2)}) collective-permute-start(bf16[8,64,3840]{2,1,0:T(8,128)(2,1)} %maximum_select_fusion.9), channel_id=1, source_target_pairs={{0,8},{2,10},{4,12},{6,14},{8,0},{10,2},{12,4},{14,6},{16,24},{18,... | collective-permute-start | bytes 11796488 | tf_op jit(solution)/shard_map/ppermute | solution.py:101
  117.4 2.2 copy-start.7
  119.8 2.1 copy-start.1
  140.2 67.6 %copy-start.2 = (bf16[2048,1024]{1,0:T(8,128)(2,1)S(1)}, bf16[2048,1024]{1,0:T(8,128)(2,1)}, u32[]{:S(2)}) copy-start(bf16[2048,1024]{1,0:T(8,128)(2,1)} %copy-done.1) | copy-start | bytes 12582916
  205.0 340.4 %collective-permute-start.5 = (bf16[8,128,3840]{2,1,0:T(8,128)(2,1)}, bf16[8,128,3840]{2,1,0:T(8,128)(2,1)}, u32[]{:S(2)}, u32[]{:S(2)}) collective-permute-start(bf16[8,128,3840]{2,1,0:T(8,128)(2,1)} %maximum_select_fusion.6), channel_id=1, source_target_pairs={{0,16},{2,18},{4,20},{6,22},{8,24},{10,26},{12,28},{14,30},{16,0},... | collective-permute-start | bytes 23592968 | tf_op jit(solution)/shard_map/ppermute | solution.py:101
  244.3 16.7 %copy-start.6 = (bf16[1536,1024]{0,1:T(8,128)(2,1)S(1)}, bf16[1536,1024]{0,1:T(8,128)(2,1)}, u32[]{:S(2)}) copy-start(bf16[1536,1024]{0,1:T(8,128)(2,1)} %copy.44) | copy-start | bytes 9437188
  273.9 271.5 %copy-start.8 = (bf16[512,8,256]{2,0,1:T(8,128)(2,1)S(1)}, bf16[512,8,256]{2,0,1:T(8,128)(2,1)}, u32[]{:S(2)}) copy-start(bf16[512,8,256]{2,0,1:T(8,128)(2,1)} %copy.51) | copy-start | bytes 6291460
  568.7 98.0 %copy-start.9 = (f32[3840]{0:T(1024)S(1)}, f32[3840]{0:T(1024)}, u32[]{:S(2)}) copy-start(f32[3840]{0:T(1024)} %param.10) | copy-start | bytes 46084
  663.6 3.3 copy-start.3
Sparse Core Ops, SparseCore 0:
  568.9 94.7 reduce-scatter.1
